TPU v7x, 512 devices: a whole 4x8x8 slice. The times are simulated.
512 devices in a mesh: hx: 32 (over x, z), hy: 16 (over y, core).
Axes of the slice: x: 4, y: 8, z: 8, core: 2. Of those that a mesh axis runs over, the one named last changes fastest.
Arguments:
- source: float32 [2048, 2048], P('hx', 'hy'), may hold values from -27 to 27
- coeffs: float32 [65, 65], replicated, may hold values from -0.13 to 0.13
- row_factor: float32 [2048, 2048], P('hx'), may hold values from -0.075 to 0.575
- col_factor: float32 [2048, 2048], P(None, 'hy'), may hold values from -0.075 to 0.575
- tile_mask: int32 [8, 8], replicated, may hold values 0 or 1
Outputs:
- solution: float32 [2048, 2048], P('hx', 'hy')
- norm_values: float32 [8], replicated
Inputs may be any that keep to these rules, and one draw needn't show every extreme that they name: tile_mask[a, b] is 1 where the tile of rows a * 256 onward and columns b * 256 onward carries a block coupling, else 0.
All inputs are finite; a program needn't handle non-finite values.
Results may differ from a plain program's by a relative error of at most 0.0003.
Values sent between devices are 32-bit elements; how exact they have to be, the bound alone decides.
A program may use at most 64 MiB of HBM per device.

v0:
```python
import functools

import jax
import jax.numpy as jnp
import ml_dtypes
import numpy as np
from jax import lax
from jax.experimental import pallas as pl
from jax.experimental.pallas import tpu as pltpu
from jax.sharding import PartitionSpec as P

TILE = 256
BAND = 32
ITERS = 8
ROWS = 64
COLS = 128
GROUP = TILE // ROWS
LONG_ROWS = ROWS + 2 * BAND
LONG_COLS = COLS + 2 * BAND
HALF = LONG_COLS // 2 + 1
Z_SIZE = 8
STEP = 0.25
TINY = 1e-06
MESH = pl.DeviceIdType.MESH
F32 = jnp.float32
BF16 = jnp.bfloat16


def split_table(table):
    high = table.astype(np.float32).astype(ml_dtypes.bfloat16)
    low = (table - high.astype(np.float64)).astype(np.float32).astype(ml_dtypes.bfloat16)
    return np.concatenate([high, low], axis=0)


def tables():
    lane = np.arange(COLS)
    freq_col = np.arange(COLS)
    kept = (freq_col < HALF).astype(np.float64)
    place = np.concatenate([lane + BAND, np.where(lane < BAND, lane + BAND + COLS, lane - (COLS - BAND))])
    used = np.concatenate([np.ones(COLS), ((lane < BAND) | (lane >= COLS - BAND)).astype(np.float64)])
    angle = 2 * np.pi * ((place[:, None] * freq_col[None, :]) % LONG_COLS) / LONG_COLS
    weight = used[:, None] * kept[None, :]
    col_forward = np.concatenate([np.cos(angle) * weight, -np.sin(angle) * weight], axis=1)
    tap = np.arange(LONG_ROWS)
    angle = 2 * np.pi * ((tap[:, None] * freq_col[None, :]) % LONG_COLS) / LONG_COLS
    weight = (tap <= 2 * BAND)[:, None] * kept[None, :]
    coeff_forward = np.concatenate([np.cos(angle) * weight, -np.sin(angle) * weight], axis=1)
    row = np.arange(LONG_ROWS)
    angle = 2 * np.pi * ((row[:, None] * row[None, :]) % LONG_ROWS) / LONG_ROWS
    row_forward = np.concatenate([np.cos(angle), np.sin(angle)], axis=0)
    target = np.arange(ROWS) + 2 * BAND
    angle = 2 * np.pi * ((target[:, None] * row[None, :]) % LONG_ROWS) / LONG_ROWS
    row_inverse = np.concatenate([np.cos(angle), np.sin(angle)], axis=0)
    target = lane + 2 * BAND
    angle = 2 * np.pi * ((freq_col[:, None] * target[None, :]) % LONG_COLS) / LONG_COLS
    scale = np.where((freq_col == 0) | (freq_col == HALF - 1), 1.0, 2.0) * kept / (LONG_ROWS * LONG_COLS)
    col_inverse = np.concatenate([np.cos(angle) * scale[:, None], -np.sin(angle) * scale[:, None]], axis=0)
    return [split_table(t) for t in (col_forward, coeff_forward, row_forward, row_inverse, col_inverse)]


def split(value):
    high = value.astype(BF16)
    return high, (value - high.astype(F32)).astype(BF16)


def dot(a, b):
    return jnp.dot(a, b, preferred_element_type=F32)


def dot_split(a, b):
    (a_high, a_low), (b_high, b_low) = a, b
    return dot(a_high, b_high) + dot(a_high, b_low) + dot(a_low, b_high)


def parts(ref):
    half = ref.shape[0] // 2
    return ref[0:half, :], ref[half:, :]


def kernel(
    sizes,
    source_hbm, coeffs_hbm, row_hbm, col_hbm, mask_ref,
    col_forward_hbm, coeff_forward_hbm, row_forward_hbm, row_inverse_hbm, col_inverse_hbm,
    out_ref, norm_ref,
    field, strips, packed, mixed_send, mixed_recv, accum, squares,
    coeffs_raw, coeffs_pad, row_tile, col_tile, row_parts, col_parts, coeff_re, coeff_im,
    col_forward, coeff_forward, row_forward, row_inverse, col_inverse,
    sum_y, sum_z, sum_x,
    local_sem, tile_send, tile_recv, edge_send, edge_recv, strip_send, strip_recv,
    mixed_send_sem, mixed_recv_sem, sum_send, sum_y_recv, sum_z_recv, sum_x_recv,
):
    n_hx, n_hy, n_z = sizes
    n_x = n_hx // n_z
    hx, hy = lax.axis_index("hx"), lax.axis_index("hy")
    place = lax.rem(hx, GROUP)
    first = hx - place
    tile_row, tile_col = hx // GROUP, hy // 2
    core = lax.rem(hy, 2)
    x, z = hx // n_z, lax.rem(hx, n_z)
    up, down, left, right = hx > 0, hx < n_hx - 1, hy > 0, hy < n_hy - 1
    own_rows = pl.ds(pl.multiple_of(BAND + place * ROWS, BAND), ROWS)

    for slot in range(2):
        field[slot, 0:BAND, :] = jnp.zeros((BAND, COLS), F32)
        field[slot, BAND + TILE :, :] = jnp.zeros((BAND, COLS), F32)
        for side in range(2):
            strips[slot, side] = jnp.zeros((4 * 8, COLS), F32)
    coeffs_pad[...] = jnp.zeros_like(coeffs_pad)

    local = [
        pltpu.make_async_copy(source_hbm, field.at[0, own_rows, :], local_sem.at[0]),
        pltpu.make_async_copy(coeffs_hbm, coeffs_raw, local_sem.at[1]),
        pltpu.make_async_copy(
            row_hbm.at[:, pl.ds(pl.multiple_of(tile_col * TILE, TILE), TILE)], row_tile, local_sem.at[2]
        ),
        pltpu.make_async_copy(
            col_hbm.at[pl.ds(pl.multiple_of(tile_row * TILE, TILE), TILE), :], col_tile, local_sem.at[3]
        ),
        pltpu.make_async_copy(col_forward_hbm, col_forward, local_sem.at[4]),
        pltpu.make_async_copy(coeff_forward_hbm, coeff_forward, local_sem.at[5]),
        pltpu.make_async_copy(row_forward_hbm, row_forward, local_sem.at[6]),
        pltpu.make_async_copy(row_inverse_hbm, row_inverse, local_sem.at[7]),
        pltpu.make_async_copy(col_inverse_hbm, col_inverse, local_sem.at[8]),
    ]
    for item in local:
        item.start()

    barrier = pltpu.get_barrier_semaphore()

    def greet(to_hx, to_hy):
        pl.semaphore_signal(barrier, inc=1, device_id=(to_hx, to_hy), device_id_type=MESH)

    def greet_y(i, carry):
        greet(hx, lax.rem(hy + i, n_hy))
        return carry

    def greet_z(i, carry):
        greet(x * n_z + lax.rem(z + i, n_z), hy)
        return carry

    def greet_x(i, carry):
        greet(lax.rem(x + i, n_x) * n_z + z, hy)
        return carry

    lax.fori_loop(1, n_hy, greet_y, 0)
    lax.fori_loop(1, n_z, greet_z, 0)
    lax.fori_loop(1, n_x, greet_x, 0)
    for there, to_hx in ((up, hx - 1), (down, hx + 1)):
        @pl.when(there)
        def _():
            greet(to_hx, hy)

            @pl.when(left)
            def _():
                greet(to_hx, hy - 1)

            @pl.when(right)
            def _():
                greet(to_hx, hy + 1)

    lane_group = lax.broadcasted_iota(jnp.int32, (8, COLS), 1) // BAND

    def pack(value):
        for half in range(2):
            to_left = to_right = None
            for g in range(4):
                start = half * BAND + 8 * g
                rolled = value[start : start + 8, :]
                if g:
                    rolled = pltpu.roll(rolled, BAND * g, axis=1)
                if to_left is None:
                    to_left = to_right = rolled
                else:
                    to_left = jnp.where(lane_group == g, rolled, to_left)
                    to_right = jnp.where(lane_group == (g + 3) % 4, rolled, to_right)
            packed[0, 8 * half : 8 * half + 8, :] = to_left
            packed[1, 8 * half : 8 * half + 8, :] = to_right

    local[0].wait()
    source = field[0, own_rows, :]
    accum[...] = source
    pack(source)

    local[2].wait()
    local[3].wait()
    active = mask_ref[tile_row, tile_col].astype(F32)
    high, low = split(row_tile[...] * active)
    row_parts[0:ROWS, :] = high
    row_parts[ROWS:, :] = low
    for which, start in enumerate((core, 1 - core)):
        high, low = split(col_tile[pl.ds(pl.multiple_of(start * COLS, COLS), COLS), :])
        col_parts[which, 0:COLS, :] = high
        col_parts[which, COLS:, :] = low
    local[1].wait()
    coeffs_pad[0 : 2 * BAND + 1, 0 : 2 * BAND + 1] = coeffs_raw[...]
    local[5].wait()
    local[6].wait()
    by_col = dot_split(split(coeffs_pad[...]), parts(coeff_forward))
    turned = dot_split(parts(row_forward), split(by_col))
    coeff_re[...] = turned[0:LONG_ROWS, 0:COLS] + turned[LONG_ROWS:, COLS:]
    coeff_im[...] = turned[0:LONG_ROWS, COLS:] - turned[LONG_ROWS:, 0:COLS]
    for i in (4, 7, 8):
        local[i].wait()

    count = (up.astype(jnp.int32) + down.astype(jnp.int32)) * (
        1 + left.astype(jnp.int32) + right.astype(jnp.int32)
    ) + (n_hy - 1 + n_z - 1 + n_x - 1)
    pl.semaphore_wait(barrier, count)

    def remote(source_ref, target_ref, send_sem, recv_sem, to_hx, to_hy):
        return pltpu.make_async_remote_copy(
            src_ref=source_ref, dst_ref=target_ref, send_sem=send_sem, recv_sem=recv_sem,
            device_id=(to_hx, to_hy), device_id_type=MESH,
        )

    def tile_copy(slot, which):
        block = field.at[slot, own_rows, :]
        return remote(block, block, tile_send.at[which], tile_recv.at[slot, place], first + which, hy)

    def tile_arrival(slot, which):
        block = field.at[slot, BAND + which * ROWS : BAND + (which + 1) * ROWS, :]
        return remote(block, block, tile_send.at[which], tile_recv.at[slot, which], first + which, hy)

    def edge_up(slot):
        return remote(
            field.at[slot, BAND : 2 * BAND, :], field.at[slot, BAND + TILE : 2 * BAND + TILE, :],
            edge_send.at[0], edge_recv.at[slot, 1], hx - 1, hy,
        )

    def edge_down(slot):
        return remote(
            field.at[slot, TILE : TILE + BAND, :], field.at[slot, 0:BAND, :],
            edge_send.at[1], edge_recv.at[slot, 0], hx + 1, hy,
        )

    def edge_arrival(slot, which):
        rows = field.at[slot, 0:BAND, :] if which == 0 else field.at[slot, BAND + TILE : 2 * BAND + TILE, :]
        return remote(rows, rows, edge_send.at[which], edge_recv.at[slot, which], hx, hy)

    def strip_copy(slot, side, which):
        to_hy = hy - 1 if side == 0 else hy + 1
        if which == 0:
            rows, target, sem, to_hx = packed.at[side, 0:8, :], strips.at[slot, 1 - side, 24:32, :], 2, hx - 1
        elif which == 1:
            rows, target, sem, to_hx = packed.at[side], strips.at[slot, 1 - side, 8:24, :], 1, hx
        else:
            rows, target, sem, to_hx = packed.at[side, 8:16, :], strips.at[slot, 1 - side, 0:8, :], 0, hx + 1
        return remote(rows, target, strip_send.at[side, which], strip_recv.at[slot, 1 - side, sem], to_hx, to_hy)

    def strip_arrival(slot, side, which):
        start, stop = ((0, 8), (8, 24), (24, 32))[which]
        rows = strips.at[slot, side, start:stop, :]
        return remote(rows, rows, strip_send.at[side, which], strip_recv.at[slot, side, which], hx, hy)

    def mixed_copy(slot):
        return remote(
            mixed_send, mixed_recv.at[slot], mixed_send_sem, mixed_recv_sem.at[slot], hx, hy + 1 - 2 * core
        )

    def on(conditions, action):
        if conditions:
            pl.when(functools.reduce(jnp.logical_and, conditions))(action)
        else:
            action()

    row_there = ((0, (up,)), (1, ()), (2, (down,)))
    side_there = ((0, left), (1, right))

    def all_sends(slot, act):
        for distance in (3, 2, 1):
            for step in (-distance, distance):
                which = place + step
                on([which >= 0, which < GROUP], lambda which=which: act(tile_copy(slot, which)))
        on([place == 0, up], lambda: act(edge_up(slot)))
        on([place == GROUP - 1, down], lambda: act(edge_down(slot)))
        for side, beside in side_there:
            for which, there in row_there:
                on([beside, *there], lambda side=side, which=which: act(strip_copy(slot, side, which)))

    def iteration(k, carry):
        slot = lax.rem(k, 2)
        all_sends(slot, lambda item: item.start())

        on([place == 0, up], lambda: edge_arrival(slot, 0).wait_recv())
        on([place == GROUP - 1, down], lambda: edge_arrival(slot, 1).wait_recv())
        for which in range(GROUP):
            near = [jnp.abs(place - which) == 1]
            on(near, lambda which=which: tile_arrival(slot, which).wait_recv())
        for side, beside in side_there:
            for which, there in row_there:
                on([beside, *there], lambda side=side, which=which: strip_arrival(slot, side, which).wait_recv())

        tall = field[slot, pl.ds(pl.multiple_of(place * ROWS, ROWS), LONG_ROWS), :]
        from_left, from_right = strips[slot, 0], strips[slot, 1]
        pieces = []
        for t in range(4):
            piece_left, piece_right = from_left[8 * t : 8 * t + 8, :], from_right[8 * t : 8 * t + 8, :]
            for g in range(4):
                piece = jnp.where(
                    lane_group == g, piece_right, jnp.where(lane_group == (g + 3) % 4, piece_left, 0.0)
                )
                pieces.append(pltpu.roll(piece, COLS - BAND * g, axis=1) if g else piece)
        wide = jnp.concatenate([tall, jnp.concatenate(pieces, axis=0)], axis=1)
        by_col = dot_split(split(wide), parts(col_forward))
        turned = dot_split(parts(row_forward), split(by_col))
        freq_re = turned[0:LONG_ROWS, 0:COLS] + turned[LONG_ROWS:, COLS:]
        freq_im = turned[0:LONG_ROWS, COLS:] - turned[LONG_ROWS:, 0:COLS]
        c_re, c_im = coeff_re[...], coeff_im[...]
        product = jnp.concatenate([freq_re * c_re - freq_im * c_im, freq_re * c_im + freq_im * c_re], axis=1)
        turned = dot_split(parts(row_inverse), split(product))
        back = jnp.concatenate(
            [turned[0:ROWS, 0:COLS] - turned[ROWS:, COLS:], turned[0:ROWS, COLS:] + turned[ROWS:, 0:COLS]], axis=1
        )
        band = dot_split(split(back), parts(col_inverse))

        for which in range(GROUP):
            far = [jnp.abs(place - which) > 1]
            on(far, lambda which=which: tile_arrival(slot, which).wait_recv())
        mixed = dot_split(parts(row_parts), split(field[slot, BAND : BAND + TILE, :]))
        mixed_send[...] = mixed
        mixed_copy(slot).start()
        total = band + dot_split(split(mixed), parts(col_parts.at[0]))
        mixed_copy(slot).wait_recv()
        total = total + dot_split(split(mixed_recv[slot]), parts(col_parts.at[1]))

        keep = jnp.where(k == 0, 0.0, 1.0 - STEP)
        take = jnp.where(k == 0, 1.0, STEP)
        residual = keep * field[slot, own_rows, :] - take * total
        all_sends(slot, lambda item: item.wait_send())
        mixed_copy(slot).wait_send()
        field[1 - slot, own_rows, :] = residual
        pack(residual)
        accum[...] += STEP * residual
        squares[pl.ds(k, 1), :] = jnp.sum(residual * residual, axis=0, keepdims=True)
        return carry

    lax.fori_loop(0, ITERS, iteration, 0)
    out_ref[...] = accum[...]

    def gather(total, held, recv_sem, index, size, device):
        held[index] = total

        def copy(to, at):
            return remote(
                held.at[index], held.at[at], sum_send.at[to], recv_sem.at[at], *device(to)
            )

        def start(i, carry):
            copy(lax.rem(index + i, size), index).start()
            return carry

        def wait(i, carry):
            other = lax.rem(index + i, size)
            item = remote(held.at[other], held.at[other], sum_send.at[other], recv_sem.at[other], *device(other))
            item.wait_recv()
            copy(other, index).wait_send()
            return carry

        lax.fori_loop(1, size, start, 0)
        lax.fori_loop(1, size, wait, 0)
        return jnp.sum(held[...], axis=0)

    total = gather(squares[...], sum_y, sum_y_recv, hy, n_hy, lambda to: (hx, to))
    total = gather(total, sum_z, sum_z_recv, z, n_z, lambda to: (x * n_z + to, hy))
    if n_x > 1:
        total = gather(total, sum_x, sum_x_recv, x, n_x, lambda to: (to * n_z + z, hy))
    mean = jnp.sum(total, axis=1, keepdims=True) / (ROWS * COLS * n_hx * n_hy)
    norm_ref[...] = jnp.broadcast_to(jnp.sqrt(mean + TINY), norm_ref.shape)


def local_step(sizes, source, coeffs, row_factor, col_factor, tile_mask):
    n_hx, n_hy, n_z = sizes
    constants = [jnp.asarray(t) for t in tables()]
    any_spec = pl.BlockSpec(memory_space=pl.ANY)
    vmem_spec = pl.BlockSpec(memory_space=pltpu.VMEM)
    dma = pltpu.SemaphoreType.DMA
    taps = 2 * BAND + 1
    scratch = [
        pltpu.VMEM((2, TILE + 2 * BAND, COLS), F32),
        pltpu.VMEM((2, 2, 32, COLS), F32),
        pltpu.VMEM((2, 16, COLS), F32),
        pltpu.VMEM((ROWS, COLS), F32),
        pltpu.VMEM((2, ROWS, COLS), F32),
        pltpu.VMEM((ROWS, COLS), F32),
        pltpu.VMEM((ITERS, COLS), F32),
        pltpu.VMEM((taps, taps), F32),
        pltpu.VMEM((LONG_ROWS, COLS), F32),
        pltpu.VMEM((ROWS, TILE), F32),
        pltpu.VMEM((TILE, COLS), F32),
        pltpu.VMEM((2 * ROWS, TILE), BF16),
        pltpu.VMEM((2, 2 * COLS, COLS), BF16),
        pltpu.VMEM((LONG_ROWS, COLS), F32),
        pltpu.VMEM((LONG_ROWS, COLS), F32),
        *[pltpu.VMEM(c.shape, c.dtype) for c in constants],
        pltpu.VMEM((n_hy, ITERS, COLS), F32),
        pltpu.VMEM((n_z, ITERS, COLS), F32),
        pltpu.VMEM((n_hx // n_z, ITERS, COLS), F32),
        dma((9,)),
        dma((GROUP,)), dma((2, GROUP)),
        dma((2,)), dma((2, 2)),
        dma((2, 3)), dma((2, 2, 3)),
        dma, dma((2,)),
        dma((max(n_hy, n_z),)), dma((n_hy,)), dma((n_z,)), dma((n_hx // n_z,)),
    ]
    result, norms = pl.pallas_call(
        functools.partial(kernel, sizes),
        out_shape=(jax.ShapeDtypeStruct((ROWS, COLS), F32), jax.ShapeDtypeStruct((ITERS, COLS), F32)),
        in_specs=[any_spec] * 4 + [pl.BlockSpec(memory_space=pltpu.SMEM)] + [any_spec] * 5,
        out_specs=(vmem_spec, vmem_spec),
        scratch_shapes=scratch,
        compiler_params=pltpu.CompilerParams(collective_id=0, has_side_effects=True),
        name="richardson",
    )(source, coeffs, row_factor, col_factor, tile_mask, *constants)
    return result, norms[:, 0]


def solution(mesh):
    n_hx, n_hy = mesh.shape["hx"], mesh.shape["hy"]
    sizes = (n_hx, n_hy, min(n_hx, Z_SIZE))
    in_specs = (P("hx", "hy"), P(), P("hx", None), P(None, "hy"), P())
    out_specs = (P("hx", "hy"), P())
    return jax.shard_map(
        functools.partial(local_step, sizes), mesh=mesh, in_specs=in_specs, out_specs=out_specs, check_vma=False
    )
```

profile of v0, /device:TPU:1, one launch (start us, length us, event | category | flops | bytes accessed | tf_op | source)
XLA Modules:
  0.0 88.7 jit_solution(5802335935967175117)
XLA Ops:
  0.6 85.3 %richardson.1 = (f32[64,128]{1,0:T(8,128)}, f32[8,128]{1,0:T(8,128)}) custom-call(f32[64,128]{1,0:T(8,128)} %source_hbm.1, f32[65,65]{1,0:T(8,128)} %coeffs_hbm.1, f32[64,2048]{1,0:T(8,128)} %row_hbm.1, f32[2048,128]{1,0:T(8,128)} %col_hbm.1, s32[8,8]{1,0:T(8,128)} %mask_ref.1, bf16[512,256]{1,0:T(8,128)(2,1)} %constant.10.clone.col_forward_hbm, ...), custom_call_target="tpu_custom_call" | custom-call | tf_op jit(solution)/shard_map/richardson/pallas_call | solution.py:405
  86.0 1.3 %slice_reduce_fusion = f32[8]{0:T(128)} fusion(f32[8,128]{1,0:T(8,128)} %get-tuple-element.5), kind=kLoop, calls=%fused_computation | loop fusion | bytes 64 | tf_op jit(solution)/shard_map/slice | solution.py:414
  87.3 1.4 %copy.13 = f32[64,128]{1,0:T(8,128)} copy(f32[64,128]{1,0:T(8,128)} %get-tuple-element.8) | data formatting | bytes 65536
where the time goes:
time: 88.9 us; the launch traced here: 88.7 us
  Pallas kernels  85.3 us (96%)
  local copies, waits for them, and re-layouts  2.67 us (3%)
    pallas_call x1, Pallas kernels, local_step(): pl.pallas_call(functools.partial(kernel, sizes), out_shape=(jax.ShapeDtyp...  85.3 us

commit v1 on v0

--- a/solution.py
+++ b/solution.py
@@ -19,6 +19,7 @@
 LONG_COLS = COLS + 2 * BAND
 HALF = LONG_COLS // 2 + 1
 Z_SIZE = 8
+NEAR = 1
 STEP = 0.25
 TINY = 1e-06
 MESH = pl.DeviceIdType.MESH
@@ -82,11 +83,11 @@
     source_hbm, coeffs_hbm, row_hbm, col_hbm, mask_ref,
     col_forward_hbm, coeff_forward_hbm, row_forward_hbm, row_inverse_hbm, col_inverse_hbm,
     out_ref, norm_ref,
-    field, strips, packed, mixed_send, mixed_recv, accum, squares,
-    coeffs_raw, coeffs_pad, row_tile, col_tile, row_parts, col_parts, coeff_re, coeff_im,
+    field, products, partner, strips, packed, mixed_send, mixed_recv, accum, squares,
+    coeffs_raw, coeffs_pad, row_tile, col_tile, row_near, row_far, col_parts, coeff_re, coeff_im,
     col_forward, coeff_forward, row_forward, row_inverse, col_inverse,
     sum_y, sum_z, sum_x,
-    local_sem, tile_send, tile_recv, edge_send, edge_recv, strip_send, strip_recv,
+    local_sem, tile_send, tile_recv, partner_send, partner_recv, edge_send, edge_recv, strip_send, strip_recv,
     mixed_send_sem, mixed_recv_sem, sum_send, sum_y_recv, sum_z_recv, sum_x_recv,
 ):
     n_hx, n_hy, n_z = sizes
@@ -99,10 +100,12 @@
     x, z = hx // n_z, lax.rem(hx, n_z)
     up, down, left, right = hx > 0, hx < n_hx - 1, hy > 0, hy < n_hy - 1
     own_rows = pl.ds(pl.multiple_of(BAND + place * ROWS, BAND), ROWS)
+    own_product = pl.ds(pl.multiple_of(place * ROWS, ROWS), ROWS)
+    beside_core = hy + 1 - 2 * core
 
     for slot in range(2):
-        field[slot, 0:BAND, :] = jnp.zeros((BAND, COLS), F32)
-        field[slot, BAND + TILE :, :] = jnp.zeros((BAND, COLS), F32)
+        field[slot] = jnp.zeros(field.shape[1:], F32)
+        products[slot] = jnp.zeros(products.shape[1:], F32)
         for side in range(2):
             strips[slot, side] = jnp.zeros((4 * 8, COLS), F32)
     coeffs_pad[...] = jnp.zeros_like(coeffs_pad)
@@ -184,9 +187,12 @@
     local[2].wait()
     local[3].wait()
     active = mask_ref[tile_row, tile_col].astype(F32)
-    high, low = split(row_tile[...] * active)
-    row_parts[0:ROWS, :] = high
-    row_parts[ROWS:, :] = low
+    distance = jnp.abs(lax.broadcasted_iota(jnp.int32, (ROWS, TILE), 1) // ROWS - place)
+    is_near = (distance >= 1) & (distance <= NEAR)
+    for parts_of, chosen in ((row_near, is_near), (row_far, ~is_near)):
+        high, low = split(jnp.where(chosen, row_tile[...] * active, 0.0))
+        parts_of[0:ROWS, :] = high
+        parts_of[ROWS:, :] = low
     for which, start in enumerate((core, 1 - core)):
         high, low = split(col_tile[pl.ds(pl.multiple_of(start * COLS, COLS), COLS), :])
         col_parts[which, 0:COLS, :] = high
@@ -213,12 +219,14 @@
             device_id=(to_hx, to_hy), device_id_type=MESH,
         )
 
-    def tile_copy(slot, which):
-        block = field.at[slot, own_rows, :]
+    def tile_copy(slot, which, near):
+        block = field.at[slot, own_rows, :] if near else products.at[slot, own_product, :]
         return remote(block, block, tile_send.at[which], tile_recv.at[slot, place], first + which, hy)
 
-    def tile_arrival(slot, which):
+    def tile_arrival(slot, which, near):
         block = field.at[slot, BAND + which * ROWS : BAND + (which + 1) * ROWS, :]
+        if not near:
+            block = products.at[slot, which * ROWS : (which + 1) * ROWS, :]
         return remote(block, block, tile_send.at[which], tile_recv.at[slot, which], first + which, hy)
 
     def edge_up(slot):
@@ -253,8 +261,11 @@
         return remote(rows, rows, strip_send.at[side, which], strip_recv.at[slot, side, which], hx, hy)
 
     def mixed_copy(slot):
+        return remote(mixed_send, mixed_recv.at[slot], mixed_send_sem, mixed_recv_sem.at[slot], hx, beside_core)
+
+    def partner_copy(slot):
         return remote(
-            mixed_send, mixed_recv.at[slot], mixed_send_sem, mixed_recv_sem.at[slot], hx, hy + 1 - 2 * core
+            field.at[slot, own_rows, :], partner.at[slot], partner_send, partner_recv.at[slot], hx, beside_core
         )
 
     def on(conditions, action):
@@ -266,31 +277,51 @@
     row_there = ((0, (up,)), (1, ()), (2, (down,)))
     side_there = ((0, left), (1, right))
 
-    def all_sends(slot, act):
-        for distance in (3, 2, 1):
+    def tile_sends(slot, near, act):
+        for distance in range(1, NEAR + 1) if near else range(GROUP - 1, NEAR, -1):
             for step in (-distance, distance):
                 which = place + step
-                on([which >= 0, which < GROUP], lambda which=which: act(tile_copy(slot, which)))
-        on([place == 0, up], lambda: act(edge_up(slot)))
-        on([place == GROUP - 1, down], lambda: act(edge_down(slot)))
+                on([which >= 0, which < GROUP], lambda which=which: act(tile_copy(slot, which, near)))
+
+    def tile_waits(slot, near):
+        for which in range(GROUP):
+            distance = jnp.abs(place - which)
+            chosen = [distance >= 1, distance <= NEAR] if near else [distance > NEAR]
+            on(chosen, lambda which=which: tile_arrival(slot, which, near).wait_recv())
+
+    def block_sends(slot, act):
+        act(partner_copy(slot))
+        tile_sends(slot, True, act)
         for side, beside in side_there:
             for which, there in row_there:
                 on([beside, *there], lambda side=side, which=which: act(strip_copy(slot, side, which)))
+        on([place == 0, up], lambda: act(edge_up(slot)))
+        on([place == GROUP - 1, down], lambda: act(edge_down(slot)))
 
     def iteration(k, carry):
         slot = lax.rem(k, 2)
-        all_sends(slot, lambda item: item.start())
+        block_sends(slot, lambda item: item.start())
+
+        product = dot_split(split(field[slot, own_rows, :]), parts(col_parts.at[0]))
+        partner_copy(slot).wait_recv()
+        product = product + dot_split(split(partner[slot]), parts(col_parts.at[1]))
+        products[slot, own_product, :] = product
+        tile_sends(slot, False, lambda item: item.start())
+
+        tile_waits(slot, True)
+        mixed = dot_split(parts(row_near), split(field[slot, BAND : BAND + TILE, :]))
+        mixed_send[...] = mixed
+        mixed_copy(slot).start()
+        total = dot_split(split(mixed), parts(col_parts.at[0]))
 
         on([place == 0, up], lambda: edge_arrival(slot, 0).wait_recv())
         on([place == GROUP - 1, down], lambda: edge_arrival(slot, 1).wait_recv())
-        for which in range(GROUP):
-            near = [jnp.abs(place - which) == 1]
-            on(near, lambda which=which: tile_arrival(slot, which).wait_recv())
+        tall = field[slot, pl.ds(pl.multiple_of(place * ROWS, ROWS), LONG_ROWS), :]
+        col_high, col_low = parts(col_forward)
+        by_col = dot_split(split(tall), (col_high[0:COLS], col_low[0:COLS]))
         for side, beside in side_there:
             for which, there in row_there:
                 on([beside, *there], lambda side=side, which=which: strip_arrival(slot, side, which).wait_recv())
-
-        tall = field[slot, pl.ds(pl.multiple_of(place * ROWS, ROWS), LONG_ROWS), :]
         from_left, from_right = strips[slot, 0], strips[slot, 1]
         pieces = []
         for t in range(4):
@@ -300,33 +331,29 @@
                     lane_group == g, piece_right, jnp.where(lane_group == (g + 3) % 4, piece_left, 0.0)
                 )
                 pieces.append(pltpu.roll(piece, COLS - BAND * g, axis=1) if g else piece)
-        wide = jnp.concatenate([tall, jnp.concatenate(pieces, axis=0)], axis=1)
-        by_col = dot_split(split(wide), parts(col_forward))
+        outside = jnp.concatenate(pieces, axis=0)
+        by_col = by_col + dot_split(split(outside), (col_high[COLS:], col_low[COLS:]))
         turned = dot_split(parts(row_forward), split(by_col))
         freq_re = turned[0:LONG_ROWS, 0:COLS] + turned[LONG_ROWS:, COLS:]
         freq_im = turned[0:LONG_ROWS, COLS:] - turned[LONG_ROWS:, 0:COLS]
         c_re, c_im = coeff_re[...], coeff_im[...]
-        product = jnp.concatenate([freq_re * c_re - freq_im * c_im, freq_re * c_im + freq_im * c_re], axis=1)
-        turned = dot_split(parts(row_inverse), split(product))
+        shaped = jnp.concatenate([freq_re * c_re - freq_im * c_im, freq_re * c_im + freq_im * c_re], axis=1)
+        turned = dot_split(parts(row_inverse), split(shaped))
         back = jnp.concatenate(
             [turned[0:ROWS, 0:COLS] - turned[ROWS:, COLS:], turned[0:ROWS, COLS:] + turned[ROWS:, 0:COLS]], axis=1
         )
-        band = dot_split(split(back), parts(col_inverse))
-
-        for which in range(GROUP):
-            far = [jnp.abs(place - which) > 1]
-            on(far, lambda which=which: tile_arrival(slot, which).wait_recv())
-        mixed = dot_split(parts(row_parts), split(field[slot, BAND : BAND + TILE, :]))
-        mixed_send[...] = mixed
-        mixed_copy(slot).start()
-        total = band + dot_split(split(mixed), parts(col_parts.at[0]))
+        total = total + dot_split(split(back), parts(col_inverse))
+
         mixed_copy(slot).wait_recv()
         total = total + dot_split(split(mixed_recv[slot]), parts(col_parts.at[1]))
+        tile_waits(slot, False)
+        total = total + dot_split(parts(row_far), split(products[slot]))
 
         keep = jnp.where(k == 0, 0.0, 1.0 - STEP)
         take = jnp.where(k == 0, 1.0, STEP)
         residual = keep * field[slot, own_rows, :] - take * total
-        all_sends(slot, lambda item: item.wait_send())
+        block_sends(slot, lambda item: item.wait_send())
+        tile_sends(slot, False, lambda item: item.wait_send())
         mixed_copy(slot).wait_send()
         field[1 - slot, own_rows, :] = residual
         pack(residual)
@@ -377,6 +404,8 @@
     taps = 2 * BAND + 1
     scratch = [
         pltpu.VMEM((2, TILE + 2 * BAND, COLS), F32),
+        pltpu.VMEM((2, TILE, COLS), F32),
+        pltpu.VMEM((2, ROWS, COLS), F32),
         pltpu.VMEM((2, 2, 32, COLS), F32),
         pltpu.VMEM((2, 16, COLS), F32),
         pltpu.VMEM((ROWS, COLS), F32),
@@ -388,6 +417,7 @@
         pltpu.VMEM((ROWS, TILE), F32),
         pltpu.VMEM((TILE, COLS), F32),
         pltpu.VMEM((2 * ROWS, TILE), BF16),
+        pltpu.VMEM((2 * ROWS, TILE), BF16),
         pltpu.VMEM((2, 2 * COLS, COLS), BF16),
         pltpu.VMEM((LONG_ROWS, COLS), F32),
         pltpu.VMEM((LONG_ROWS, COLS), F32),
@@ -397,6 +427,7 @@
         pltpu.VMEM((n_hx // n_z, ITERS, COLS), F32),
         dma((9,)),
         dma((GROUP,)), dma((2, GROUP)),
+        dma, dma((2,)),
         dma((2,)), dma((2, 2)),
         dma((2, 3)), dma((2, 2, 3)),
         dma, dma((2,)),

time: 88.9 us -> 79 us (0.89)
  Pallas kernels: 85.3 us -> 75.5 us
    pallas_call x1, Pallas kernels: 85.3 us -> 75.5 us  [local_step(): pl.pallas_call(functools.partial(kernel, sizes), out_shape=(jax.ShapeDtyp...]
where the time goes in v1:
time: 79 us; the launch traced here: 78.8 us
  Pallas kernels  75.5 us (96%)
  local copies, waits for them, and re-layouts  2.67 us (3%)
    pallas_call x1, Pallas kernels, local_step(): pl.pallas_call(functools.partial(kernel, sizes), out_shape=(jax.ShapeDtyp...  75.5 us

profile of v1, /device:TPU:1, one launch (start us, length us, event | category | flops | bytes accessed | tf_op | source)
XLA Modules:
  0.0 78.8 jit_solution(79668828527802798)
XLA Ops:
  0.6 75.5 %richardson.1 = (f32[64,128]{1,0:T(8,128)}, f32[8,128]{1,0:T(8,128)}) custom-call(f32[64,128]{1,0:T(8,128)} %source_hbm.1, f32[65,65]{1,0:T(8,128)} %coeffs_hbm.1, f32[64,2048]{1,0:T(8,128)} %row_hbm.1, f32[2048,128]{1,0:T(8,128)} %col_hbm.1, s32[8,8]{1,0:T(8,128)} %mask_ref.1, bf16[512,256]{1,0:T(8,128)(2,1)} %constant.10.clone.col_forward_hbm, ...), custom_call_target="tpu_custom_call" | custom-call | tf_op jit(solution)/shard_map/richardson/pallas_call | solution.py:436
  76.1 1.3 %slice_reduce_fusion = f32[8]{0:T(128)} fusion(f32[8,128]{1,0:T(8,128)} %get-tuple-element.5), kind=kLoop, calls=%fused_computation | loop fusion | bytes 64 | tf_op jit(solution)/shard_map/slice | solution.py:445
  77.4 1.4 %copy.13 = f32[64,128]{1,0:T(8,128)} copy(f32[64,128]{1,0:T(8,128)} %get-tuple-element.8) | data formatting | bytes 65536

commit v2 on v1

v2 whole, which is shorter than its diff:
```python
import functools

import jax
import jax.numpy as jnp
import ml_dtypes
import numpy as np
from jax import lax
from jax.experimental import pallas as pl
from jax.experimental.pallas import tpu as pltpu
from jax.sharding import PartitionSpec as P

TILE = 256
BAND = 32
ITERS = 8
ROWS = 64
COLS = 128
GROUP = TILE // ROWS
LONG_ROWS = ROWS + 2 * BAND
LONG_COLS = COLS + 2 * BAND
HALF = LONG_COLS // 2 + 1
NEAR = 1
STEP = 0.25
TINY = 1e-06
Z_SIZE = 8
MESH = pl.DeviceIdType.MESH
F32 = jnp.float32
BF16 = jnp.bfloat16


def split_table(table):
    high = table.astype(np.float32).astype(ml_dtypes.bfloat16)
    low = (table - high.astype(np.float64)).astype(np.float32).astype(ml_dtypes.bfloat16)
    return high, low


def tables():
    lane = np.arange(COLS)
    freq_col = np.arange(COLS)
    kept = (freq_col < HALF).astype(np.float64)
    place = np.concatenate([lane + BAND, np.where(lane < BAND, lane + BAND + COLS, lane - (COLS - BAND))])
    used = np.concatenate([np.ones(COLS), ((lane < BAND) | (lane >= COLS - BAND)).astype(np.float64)])
    angle = 2 * np.pi * ((place[:, None] * freq_col[None, :]) % LONG_COLS) / LONG_COLS
    weight = used[:, None] * kept[None, :]
    col_forward = np.concatenate([np.cos(angle) * weight, -np.sin(angle) * weight], axis=1)
    tap = np.arange(LONG_ROWS)
    angle = 2 * np.pi * ((tap[:, None] * freq_col[None, :]) % LONG_COLS) / LONG_COLS
    weight = (tap <= 2 * BAND)[:, None] * kept[None, :]
    coeff_forward = np.concatenate([np.cos(angle) * weight, -np.sin(angle) * weight], axis=1)
    row = np.arange(LONG_ROWS)
    angle = 2 * np.pi * ((row[:, None] * row[None, :]) % LONG_ROWS) / LONG_ROWS
    order = np.concatenate([row[0::2], row[1::2]])
    halves = [angle[row[odd::2], : LONG_ROWS // 2] for odd in (0, 1)]
    row_forward = np.concatenate([f(half) for half in halves for f in (np.cos, np.sin)], axis=0)
    target = np.arange(ROWS) + 2 * BAND
    angle = 2 * np.pi * ((target[:, None] * order[None, :]) % LONG_ROWS) / LONG_ROWS
    row_inverse = np.concatenate([np.cos(angle), np.sin(angle)], axis=0)
    target = lane + 2 * BAND
    angle = 2 * np.pi * ((freq_col[:, None] * target[None, :]) % LONG_COLS) / LONG_COLS
    scale = np.where((freq_col == 0) | (freq_col == HALF - 1), 1.0, 2.0) * kept / (LONG_ROWS * LONG_COLS)
    col_inverse = np.concatenate([np.cos(angle) * scale[:, None], -np.sin(angle) * scale[:, None]], axis=0)
    high, low = split_table(row_forward)
    row_forward = np.concatenate([high, high, low, low], axis=1)
    return [
        np.concatenate(split_table(col_forward), axis=0),
        np.concatenate(split_table(coeff_forward), axis=0),
        row_forward,
        np.concatenate(split_table(row_inverse), axis=1),
        np.concatenate(split_table(col_inverse), axis=1),
    ]


def split(value):
    high = value.astype(BF16)
    return high, (value - high.astype(F32)).astype(BF16)


def dot(a, b):
    return jnp.dot(a, b, preferred_element_type=F32)


def beside(*values):
    return jnp.concatenate(values, axis=1)


def below(*values):
    return jnp.concatenate(values, axis=0)


def dot_rows(a, b):
    (a_high, a_low), (b_high, b_low) = a, b
    both = dot(below(a_high, a_low), b_high)
    count = a_high.shape[0]
    return both[0:count] + both[count:] + dot(a_high, b_low)


def dot_small(a, b):
    both = dot(a, b)
    return both[:, 0:COLS] + both[:, COLS:]


def dot_deep(a, b):
    both = dot(a, b)
    count = a.shape[0] // 2
    return both[0:count, 0:COLS] + (both[0:count, COLS:] + both[count:, 0:COLS])


def transform_rows(value, table):
    half = LONG_ROWS // 2
    top, bottom = value[0:half], value[half:]
    parts_re, parts_im = [], []
    for at, both in ((0, top + bottom), (LONG_ROWS, top - bottom)):
        high, low = split(both)
        turned = dot(table[at : at + LONG_ROWS, :], below(high, low, high, low))
        cosine, sine = turned[0:half], turned[half:]
        parts_re.append(cosine[:, 0:COLS] + sine[:, COLS:])
        parts_im.append(cosine[:, COLS:] - sine[:, 0:COLS])
    return below(*parts_re), below(*parts_im)


def parts(ref):
    half = ref.shape[0] // 2
    return ref[0:half, :], ref[half:, :]


def kernel(
    sizes,
    source_hbm, coeffs_hbm, row_hbm, col_hbm, mask_hbm,
    col_forward_hbm, coeff_forward_hbm, row_forward_hbm, row_inverse_hbm, col_inverse_hbm,
    out_ref, norm_ref,
    field, product_send, far, partner, strips, packed, mixed_send, mixed_recv, accum, squares,
    mask, coeffs_raw, coeffs_pad, row_tile, col_tile, row_near, row_far, col_parts, coeff_re, coeff_im,
    col_forward, coeff_forward, row_forward, row_inverse, col_inverse,
    sum_y, sum_x,
    local_sem, tile_send, tile_recv, partner_send, partner_recv, edge_send, edge_recv, strip_send, strip_recv,
    mixed_send_sem, mixed_recv_sem, sum_send, sum_y_recv, sum_x_recv,
):
    n_hx, n_hy = sizes
    n_z = min(n_hx, Z_SIZE)
    n_x = n_hx // n_z
    hx, hy = lax.axis_index("hx"), lax.axis_index("hy")
    place = lax.rem(hx, GROUP)
    first = hx - place
    tile_row, tile_col = hx // GROUP, hy // 2
    core = lax.rem(hy, 2)
    x, z = hx // n_z, lax.rem(hx, n_z)
    up, down, left, right = hx > 0, hx < n_hx - 1, hy > 0, hy < n_hy - 1
    own_rows = pl.ds(pl.multiple_of(BAND + place * ROWS, BAND), ROWS)
    own_far = pl.ds(pl.multiple_of(lax.rem(place, 2) * ROWS, ROWS), ROWS)
    far_first = jnp.where(place < 2, 2, 0)
    beside_core = hy + 1 - 2 * core

    for slot in range(2):
        field[slot] = jnp.zeros(field.shape[1:], F32)
        far[slot] = jnp.zeros(far.shape[1:], F32)
        for side in range(2):
            strips[slot, side] = jnp.zeros((4 * 8, COLS), F32)
    coeffs_pad[...] = jnp.zeros_like(coeffs_pad)

    local = [
        pltpu.make_async_copy(source_hbm, field.at[0, own_rows, :], local_sem.at[0]),
        pltpu.make_async_copy(coeffs_hbm, coeffs_raw, local_sem.at[1]),
        pltpu.make_async_copy(
            row_hbm.at[:, pl.ds(pl.multiple_of(tile_col * TILE, TILE), TILE)], row_tile, local_sem.at[2]
        ),
        pltpu.make_async_copy(
            col_hbm.at[pl.ds(pl.multiple_of(tile_row * TILE, TILE), TILE), :], col_tile, local_sem.at[3]
        ),
        pltpu.make_async_copy(col_forward_hbm, col_forward, local_sem.at[4]),
        pltpu.make_async_copy(coeff_forward_hbm, coeff_forward, local_sem.at[5]),
        pltpu.make_async_copy(row_forward_hbm, row_forward, local_sem.at[6]),
        pltpu.make_async_copy(row_inverse_hbm, row_inverse, local_sem.at[7]),
        pltpu.make_async_copy(col_inverse_hbm, col_inverse, local_sem.at[8]),
        pltpu.make_async_copy(mask_hbm, mask, local_sem.at[9]),
    ]
    for item in local:
        item.start()

    barrier = pltpu.get_barrier_semaphore()

    def greet(to_hx, to_hy):
        pl.semaphore_signal(barrier, inc=1, device_id=(to_hx, to_hy), device_id_type=MESH)

    def greet_y(i, carry):
        greet(hx, lax.rem(hy + i, n_hy))
        return carry

    def greet_z(i, carry):
        greet(x * n_z + lax.rem(z + i, n_z), hy)
        return carry

    def greet_x(i, carry):
        greet(lax.rem(x + i, n_x) * n_z + z, hy)
        return carry

    lax.fori_loop(1, n_hy, greet_y, 0)
    lax.fori_loop(1, n_z, greet_z, 0)
    lax.fori_loop(1, n_x, greet_x, 0)
    for there, to_hx in ((up, hx - 1), (down, hx + 1)):
        @pl.when(there)
        def _():
            greet(to_hx, hy)

            @pl.when(left)
            def _():
                greet(to_hx, hy - 1)

            @pl.when(right)
            def _():
                greet(to_hx, hy + 1)

    lane_group = lax.broadcasted_iota(jnp.int32, (8, COLS), 1) // BAND

    def pack(slot, value):
        for half in range(2):
            to_left = to_right = None
            for g in range(4):
                start = half * BAND + 8 * g
                rolled = value[start : start + 8, :]
                if g:
                    rolled = pltpu.roll(rolled, BAND * g, axis=1)
                if to_left is None:
                    to_left = to_right = rolled
                else:
                    to_left = jnp.where(lane_group == g, rolled, to_left)
                    to_right = jnp.where(lane_group == (g + 3) % 4, rolled, to_right)
            packed[slot, 0, 8 * half : 8 * half + 8, :] = to_left
            packed[slot, 1, 8 * half : 8 * half + 8, :] = to_right

    local[0].wait()
    accum[...] = jnp.zeros_like(accum)

    count = (up.astype(jnp.int32) + down.astype(jnp.int32)) * (
        1 + left.astype(jnp.int32) + right.astype(jnp.int32)
    ) + (n_hy - 1 + n_z - 1 + n_x - 1)
    pl.semaphore_wait(barrier, count)

    def prepare():
        local[2].wait()
        local[3].wait()
        local[9].wait()
        active = mask[tile_row, tile_col].astype(F32)
        def distance(width, start):
            return jnp.abs(lax.broadcasted_iota(jnp.int32, (ROWS, width), 1) // ROWS + (start - place))

        far_cols = row_tile[:, pl.ds(pl.multiple_of(far_first * ROWS, 2 * ROWS), 2 * ROWS)]
        for parts_of, value, chosen in (
            (row_near, row_tile[...], distance(TILE, 0) <= NEAR),
            (row_far, far_cols, distance(2 * ROWS, far_first) > NEAR),
        ):
            high, low = split(jnp.where(chosen, value * active, 0.0))
            parts_of[...] = below(high, low) if parts_of is row_near else beside(high, low)
        for which, start in enumerate((core, 1 - core)):
            high, low = split(col_tile[pl.ds(pl.multiple_of(start * COLS, COLS), COLS), :])
            col_parts[which, 0:COLS, :] = beside(high, low)
            col_parts[which, COLS:, :] = beside(high, low)
        local[1].wait()
        coeffs_pad[0 : 2 * BAND + 1, 0 : 2 * BAND + 1] = coeffs_raw[...]
        local[5].wait()
        local[6].wait()
        by_col = dot_rows(split(coeffs_pad[...]), parts(coeff_forward))
        coeff_re[...], coeff_im[...] = transform_rows(by_col, row_forward)
        for i in (4, 7, 8):
            local[i].wait()

    def remote(source_ref, target_ref, send_sem, recv_sem, to_hx, to_hy):
        return pltpu.make_async_remote_copy(
            src_ref=source_ref, dst_ref=target_ref, send_sem=send_sem, recv_sem=recv_sem,
            device_id=(to_hx, to_hy), device_id_type=MESH,
        )

    def tile_copy(slot, which, near):
        block = field.at[slot, own_rows, :]
        source_ref, target_ref = (block, block) if near else (product_send.at[slot], far.at[slot, own_far, :])
        return remote(source_ref, target_ref, tile_send.at[slot, which], tile_recv.at[slot, place], first + which, hy)

    def tile_arrival(slot, which, near):
        if near:
            block = field.at[slot, BAND + which * ROWS : BAND + (which + 1) * ROWS, :]
        else:
            block = far.at[slot, which % 2 * ROWS : (which % 2 + 1) * ROWS, :]
        return remote(block, block, tile_send.at[slot, which], tile_recv.at[slot, which], first + which, hy)

    def edge_up(slot):
        return remote(
            field.at[slot, BAND : 2 * BAND, :], field.at[slot, BAND + TILE : 2 * BAND + TILE, :],
            edge_send.at[slot, 0], edge_recv.at[slot, 1], hx - 1, hy,
        )

    def edge_down(slot):
        return remote(
            field.at[slot, TILE : TILE + BAND, :], field.at[slot, 0:BAND, :],
            edge_send.at[slot, 1], edge_recv.at[slot, 0], hx + 1, hy,
        )

    def edge_arrival(slot, which):
        rows = field.at[slot, 0:BAND, :] if which == 0 else field.at[slot, BAND + TILE : 2 * BAND + TILE, :]
        return remote(rows, rows, edge_send.at[slot, which], edge_recv.at[slot, which], hx, hy)

    def strip_copy(slot, side, which):
        to_hy = hy - 1 if side == 0 else hy + 1
        if which == 0:
            rows, target, sem, to_hx = packed.at[slot, side, 0:8, :], strips.at[slot, 1 - side, 24:32, :], 2, hx - 1
        elif which == 1:
            rows, target, sem, to_hx = packed.at[slot, side], strips.at[slot, 1 - side, 8:24, :], 1, hx
        else:
            rows, target, sem, to_hx = packed.at[slot, side, 8:16, :], strips.at[slot, 1 - side, 0:8, :], 0, hx + 1
        return remote(rows, target, strip_send.at[slot, side, which], strip_recv.at[slot, 1 - side, sem], to_hx, to_hy)

    def strip_arrival(slot, side, which):
        start, stop = ((0, 8), (8, 24), (24, 32))[which]
        rows = strips.at[slot, side, start:stop, :]
        return remote(rows, rows, strip_send.at[slot, side, which], strip_recv.at[slot, side, which], hx, hy)

    def mixed_copy(slot):
        return remote(mixed_send.at[slot], mixed_recv.at[slot], mixed_send_sem.at[slot], mixed_recv_sem.at[slot], hx, beside_core)

    def partner_copy(slot):
        return remote(
            field.at[slot, own_rows, :], partner.at[slot], partner_send.at[slot], partner_recv.at[slot], hx, beside_core
        )

    def on(conditions, action):
        if conditions:
            pl.when(functools.reduce(jnp.logical_and, conditions))(action)
        else:
            action()

    row_there = ((0, (up,)), (1, ()), (2, (down,)))
    side_there = ((0, left), (1, right))

    def tile_sends(slot, near, act):
        for distance in range(1, NEAR + 1) if near else range(GROUP - 1, NEAR, -1):
            for step in (-distance, distance):
                which = place + step
                on([which >= 0, which < GROUP], lambda which=which: act(tile_copy(slot, which, near)))

    def tile_waits(slot, near):
        for which in range(GROUP):
            distance = jnp.abs(place - which)
            chosen = [distance >= 1, distance <= NEAR] if near else [distance > NEAR]
            on(chosen, lambda which=which: tile_arrival(slot, which, near).wait_recv())

    def edge_sends(slot, act):
        on([place == 0, up], lambda: act(edge_up(slot)))
        on([place == GROUP - 1, down], lambda: act(edge_down(slot)))

    def strip_sends(slot, act):
        for which, there in (row_there[0], row_there[2], row_there[1]):
            for side, next_to in side_there:
                on([next_to, *there], lambda side=side, which=which: act(strip_copy(slot, side, which)))

    def gain(k, value):
        accum[...] += jnp.where(k == 0, 1.0, STEP) * value
        squares[pl.ds(k + ITERS - 1, 1), :] = jnp.sum(value * value, axis=0, keepdims=True)

    def begin(item):
        item.start()

    def finish(item):
        item.wait_send()

    def all_sent(slot):
        partner_copy(slot).wait_send()
        mixed_copy(slot).wait_send()
        edge_sends(slot, finish)
        tile_sends(slot, True, finish)
        strip_sends(slot, finish)
        tile_sends(slot, False, finish)

    def iteration(k, carry):
        slot = lax.rem(k, 2)
        partner_copy(slot).start()
        edge_sends(slot, begin)
        tile_sends(slot, True, begin)
        value = field[slot, own_rows, :]
        pack(slot, value)
        strip_sends(slot, begin)

        pl.when(k == 0)(prepare)

        product = dot_small(beside(*split(value)), col_parts[0])
        gain(k, value)
        partner_copy(slot).wait_recv()
        product_send[slot] = product + dot_small(beside(*split(partner[slot])), col_parts[1])
        tile_sends(slot, False, begin)

        tile_waits(slot, True)
        mixed = dot_deep(row_near[...], beside(*split(field[slot, BAND : BAND + TILE, :])))
        mixed_send[slot] = mixed
        mixed_copy(slot).start()
        total = dot_small(beside(*split(mixed)), col_parts[0])

        on([place == 0, up], lambda: edge_arrival(slot, 0).wait_recv())
        on([place == GROUP - 1, down], lambda: edge_arrival(slot, 1).wait_recv())
        tall = field[slot, pl.ds(pl.multiple_of(place * ROWS, ROWS), LONG_ROWS), :]
        for side, next_to in side_there:
            for which, there in row_there:
                on([next_to, *there], lambda side=side, which=which: strip_arrival(slot, side, which).wait_recv())
        from_left, from_right = strips[slot, 0], strips[slot, 1]
        pieces = []
        for t in range(4):
            piece_left, piece_right = from_left[8 * t : 8 * t + 8, :], from_right[8 * t : 8 * t + 8, :]
            for g in range(4):
                piece = jnp.where(
                    lane_group == g, piece_right, jnp.where(lane_group == (g + 3) % 4, piece_left, 0.0)
                )
                pieces.append(pltpu.roll(piece, COLS - BAND * g, axis=1) if g else piece)
        by_col = dot_rows(split(beside(tall, below(*pieces))), parts(col_forward))
        freq_re, freq_im = transform_rows(by_col, row_forward)
        c_re, c_im = coeff_re[...], coeff_im[...]
        high, low = split(beside(freq_re * c_re - freq_im * c_im, freq_re * c_im + freq_im * c_re))
        turned = dot(row_inverse[...], below(high, high)) + dot(row_inverse[:, 0:LONG_ROWS], low)
        cosine, sine = turned[0:ROWS], turned[ROWS:]
        back = beside(cosine[:, 0:COLS] - sine[:, COLS:], cosine[:, COLS:] + sine[:, 0:COLS])
        total = total + dot_deep(below(*split(back)), col_inverse[...])

        mixed_copy(slot).wait_recv()
        total = total + dot_small(beside(*split(mixed_recv[slot])), col_parts[1])
        pl.when(k > 0)(lambda: all_sent(1 - slot))
        keep = jnp.where(k == 0, 0.0, 1.0 - STEP)
        take = jnp.where(k == 0, 1.0, STEP)
        total = keep * value - take * total
        tile_waits(slot, False)
        field[1 - slot, own_rows, :] = total - take * dot_small(row_far[...], below(*[beside(*split(far[slot]))] * 2))
        return carry

    lax.fori_loop(0, ITERS, iteration, 0)
    gain(ITERS, field[ITERS % 2, own_rows, :])
    out_ref[...] = accum[...]
    all_sent((ITERS - 1) % 2)

    def gather(total, held, recv_sem, index, size, device):
        held[index] = total

        def copy(to, at):
            return remote(
                held.at[index], held.at[at], sum_send.at[to], recv_sem.at[at], *device(to)
            )

        def start(i, carry):
            copy(lax.rem(index + i, size), index).start()
            return carry

        def wait(i, carry):
            other = lax.rem(index + i, size)
            item = remote(held.at[other], held.at[other], sum_send.at[other], recv_sem.at[other], *device(other))
            item.wait_recv()
            copy(other, index).wait_send()
            return carry

        lax.fori_loop(1, size, start, 0)
        lax.fori_loop(1, size, wait, 0)
        return jnp.sum(held[...], axis=0)

    total = gather(squares[ITERS:, :], sum_y, sum_y_recv, hy, n_hy, lambda to: (hx, to))
    total = gather(total, sum_x.at[0:n_z], sum_x_recv.at[0], z, n_z, lambda to: (x * n_z + to, hy))
    if n_x > 1:
        total = gather(total, sum_x.at[n_z : n_z + n_x], sum_x_recv.at[1], x, n_x, lambda to: (to * n_z + z, hy))
    mean = jnp.sum(total, axis=1, keepdims=True) / (ROWS * COLS * n_hx * n_hy)
    norm_ref[...] = jnp.broadcast_to(jnp.sqrt(mean + TINY), norm_ref.shape)


def local_step(sizes, source, coeffs, row_factor, col_factor, tile_mask):
    n_hx, n_hy = sizes
    constants = [jnp.asarray(t) for t in tables()]
    any_spec = pl.BlockSpec(memory_space=pl.ANY)
    vmem_spec = pl.BlockSpec(memory_space=pltpu.VMEM)
    dma = pltpu.SemaphoreType.DMA
    taps = 2 * BAND + 1
    scratch = [
        pltpu.VMEM((2, TILE + 2 * BAND, COLS), F32),
        pltpu.VMEM((2, ROWS, COLS), F32),
        pltpu.VMEM((2, 2 * ROWS, COLS), F32),
        pltpu.VMEM((2, ROWS, COLS), F32),
        pltpu.VMEM((2, 2, 32, COLS), F32),
        pltpu.VMEM((2, 2, 16, COLS), F32),
        pltpu.VMEM((2, ROWS, COLS), F32),
        pltpu.VMEM((2, ROWS, COLS), F32),
        pltpu.VMEM((ROWS, COLS), F32),
        pltpu.VMEM((2 * ITERS, COLS), F32),
        pltpu.SMEM((n_hx // GROUP, n_hy // 2), jnp.int32),
        pltpu.VMEM((taps, taps), F32),
        pltpu.VMEM((LONG_ROWS, COLS), F32),
        pltpu.VMEM((ROWS, TILE), F32),
        pltpu.VMEM((TILE, COLS), F32),
        pltpu.VMEM((2 * ROWS, TILE), BF16),
        pltpu.VMEM((ROWS, 4 * ROWS), BF16),
        pltpu.VMEM((2, 2 * COLS, 2 * COLS), BF16),
        pltpu.VMEM((LONG_ROWS, COLS), F32),
        pltpu.VMEM((LONG_ROWS, COLS), F32),
        *[pltpu.VMEM(c.shape, c.dtype) for c in constants],
        pltpu.VMEM((n_hy, ITERS, COLS), F32),
        pltpu.VMEM((n_hx, ITERS, COLS), F32),
        dma((10,)),
        dma((2, GROUP)), dma((2, GROUP)),
        dma((2,)), dma((2,)),
        dma((2, 2)), dma((2, 2)),
        dma((2, 2, 3)), dma((2, 2, 3)),
        dma((2,)), dma((2,)),
        dma((max(n_hy, n_hx),)), dma((n_hy,)), dma((2, n_hx)),
    ]
    result, norms = pl.pallas_call(
        functools.partial(kernel, sizes),
        out_shape=(pltpu.VMEM((ROWS, COLS), F32), pltpu.VMEM((ITERS, COLS), F32)),
        in_specs=[any_spec] * 10,
        out_specs=(vmem_spec, vmem_spec),
        scratch_shapes=scratch,
        compiler_params=pltpu.CompilerParams(collective_id=0, has_side_effects=True),
        name="richardson",
    )(source, coeffs, row_factor, col_factor, tile_mask, *constants)
    return result, norms[:, 0]


def solution(mesh):
    n_hx, n_hy = mesh.shape["hx"], mesh.shape["hy"]
    sizes = (n_hx, n_hy)
    in_specs = (P("hx", "hy"), P(), P("hx", None), P(None, "hy"), P())
    out_specs = (P("hx", "hy"), P())
    return jax.shard_map(
        functools.partial(local_step, sizes), mesh=mesh, in_specs=in_specs, out_specs=out_specs, check_vma=False
    )
```

time: 79 us -> 76.2 us (0.965)
  local copies, waits for them, and re-layouts: 2.67 us -> 1.24 us
  Pallas kernels: 75.5 us -> 74.2 us
    pallas_call x1, Pallas kernels: 75.5 us -> 74.2 us  [local_step(): pl.pallas_call(functools.partial(kernel, sizes), out_shape=(pltpu.VMEM((R...]
where the time goes in v2:
time: 76.2 us; the launch traced here: 76.1 us
  Pallas kernels  74.2 us (97%)
  local copies, waits for them, and re-layouts  1.24 us (2%)
    pallas_call x1, Pallas kernels, local_step(): pl.pallas_call(functools.partial(kernel, sizes), out_shape=(pltpu.VMEM((R...  74.2 us

profile of v2, /device:TPU:1, one launch (start us, length us, event | category | flops | bytes accessed | tf_op | source)
XLA Modules:
  0.0 76.1 jit_solution(1285903216120746604)
XLA Ops:
  0.6 74.2 %richardson.1 = (f32[64,128]{1,0:T(8,128)S(1)}, f32[8,128]{1,0:T(8,128)S(1)}) custom-call(f32[64,128]{1,0:T(8,128)} %source_hbm.1, f32[65,65]{1,0:T(8,128)} %coeffs_hbm.1, f32[64,2048]{1,0:T(8,128)} %row_hbm.1, f32[2048,128]{1,0:T(8,128)} %col_hbm.1, s32[8,8]{1,0:T(8,128)} %mask_hbm.1, bf16[512,256]{1,0:T(8,128)(2,1)} %constant.10.clone.col_forward_hbm, ...), custom_call_target="tpu_custom_call" | custom-call | tf_op jit(solution)/shard_map/richardson/pallas_call | solution.py:502
  74.8 0.6 copy.13
  75.4 0.6 slice_reduce_fusion

commit v3 on v2

--- a/solution.py
+++ b/solution.py
@@ -229,30 +229,31 @@
     local[0].wait()
     accum[...] = jnp.zeros_like(accum)
 
+    local[2].wait()
+    local[3].wait()
+    local[9].wait()
+    active = mask[tile_row, tile_col].astype(F32)
+    def distance(width, start):
+        return jnp.abs(lax.broadcasted_iota(jnp.int32, (ROWS, width), 1) // ROWS + (start - place))
+
+    far_cols = row_tile[:, pl.ds(pl.multiple_of(far_first * ROWS, 2 * ROWS), 2 * ROWS)]
+    for parts_of, value, chosen in (
+        (row_near, row_tile[...], distance(TILE, 0) <= NEAR),
+        (row_far, far_cols, distance(2 * ROWS, far_first) > NEAR),
+    ):
+        high, low = split(jnp.where(chosen, value * active, 0.0))
+        parts_of[...] = below(high, low) if parts_of is row_near else beside(high, low)
+    for which, start in enumerate((core, 1 - core)):
+        high, low = split(col_tile[pl.ds(pl.multiple_of(start * COLS, COLS), COLS), :])
+        col_parts[which, 0:COLS, :] = beside(high, low)
+        col_parts[which, COLS:, :] = beside(high, low)
+
     count = (up.astype(jnp.int32) + down.astype(jnp.int32)) * (
         1 + left.astype(jnp.int32) + right.astype(jnp.int32)
     ) + (n_hy - 1 + n_z - 1 + n_x - 1)
     pl.semaphore_wait(barrier, count)
 
     def prepare():
-        local[2].wait()
-        local[3].wait()
-        local[9].wait()
-        active = mask[tile_row, tile_col].astype(F32)
-        def distance(width, start):
-            return jnp.abs(lax.broadcasted_iota(jnp.int32, (ROWS, width), 1) // ROWS + (start - place))
-
-        far_cols = row_tile[:, pl.ds(pl.multiple_of(far_first * ROWS, 2 * ROWS), 2 * ROWS)]
-        for parts_of, value, chosen in (
-            (row_near, row_tile[...], distance(TILE, 0) <= NEAR),
-            (row_far, far_cols, distance(2 * ROWS, far_first) > NEAR),
-        ):
-            high, low = split(jnp.where(chosen, value * active, 0.0))
-            parts_of[...] = below(high, low) if parts_of is row_near else beside(high, low)
-        for which, start in enumerate((core, 1 - core)):
-            high, low = split(col_tile[pl.ds(pl.multiple_of(start * COLS, COLS), COLS), :])
-            col_parts[which, 0:COLS, :] = beside(high, low)
-            col_parts[which, COLS:, :] = beside(high, low)
         local[1].wait()
         coeffs_pad[0 : 2 * BAND + 1, 0 : 2 * BAND + 1] = coeffs_raw[...]
         local[5].wait()
@@ -376,13 +377,13 @@
         pack(slot, value)
         strip_sends(slot, begin)
 
-        pl.when(k == 0)(prepare)
-
         product = dot_small(beside(*split(value)), col_parts[0])
         gain(k, value)
         partner_copy(slot).wait_recv()
         product_send[slot] = product + dot_small(beside(*split(partner[slot])), col_parts[1])
         tile_sends(slot, False, begin)
+
+        pl.when(k == 0)(prepare)
 
         tile_waits(slot, True)
         mixed = dot_deep(row_near[...], beside(*split(field[slot, BAND : BAND + TILE, :])))
@@ -452,12 +453,14 @@
         lax.fori_loop(1, size, wait, 0)
         return jnp.sum(held[...], axis=0)
 
-    total = gather(squares[ITERS:, :], sum_y, sum_y_recv, hy, n_hy, lambda to: (hx, to))
+    row, col = (lax.broadcasted_iota(jnp.int32, (ITERS, COLS), axis) for axis in (0, 1))
+    sums = jnp.sum(squares[ITERS:, :], axis=1, keepdims=True)
+    total = jnp.sum(jnp.where(row == col, sums, 0.0), axis=0, keepdims=True)
+    total = gather(total, sum_y, sum_y_recv, hy, n_hy, lambda to: (hx, to))
     total = gather(total, sum_x.at[0:n_z], sum_x_recv.at[0], z, n_z, lambda to: (x * n_z + to, hy))
     if n_x > 1:
         total = gather(total, sum_x.at[n_z : n_z + n_x], sum_x_recv.at[1], x, n_x, lambda to: (to * n_z + z, hy))
-    mean = jnp.sum(total, axis=1, keepdims=True) / (ROWS * COLS * n_hx * n_hy)
-    norm_ref[...] = jnp.broadcast_to(jnp.sqrt(mean + TINY), norm_ref.shape)
+    norm_ref[...] = jnp.sqrt(total / (ROWS * COLS * n_hx * n_hy) + TINY)
 
 
 def local_step(sizes, source, coeffs, row_factor, col_factor, tile_mask):
@@ -489,8 +492,8 @@
         pltpu.VMEM((LONG_ROWS, COLS), F32),
         pltpu.VMEM((LONG_ROWS, COLS), F32),
         *[pltpu.VMEM(c.shape, c.dtype) for c in constants],
-        pltpu.VMEM((n_hy, ITERS, COLS), F32),
-        pltpu.VMEM((n_hx, ITERS, COLS), F32),
+        pltpu.VMEM((n_hy, 1, COLS), F32),
+        pltpu.VMEM((n_hx, 1, COLS), F32),
         dma((10,)),
         dma((2, GROUP)), dma((2, GROUP)),
         dma((2,)), dma((2,)),
@@ -501,14 +504,14 @@
     ]
     result, norms = pl.pallas_call(
         functools.partial(kernel, sizes),
-        out_shape=(pltpu.VMEM((ROWS, COLS), F32), pltpu.VMEM((ITERS, COLS), F32)),
+        out_shape=(pltpu.VMEM((ROWS, COLS), F32), pltpu.VMEM((1, COLS), F32)),
         in_specs=[any_spec] * 10,
         out_specs=(vmem_spec, vmem_spec),
         scratch_shapes=scratch,
         compiler_params=pltpu.CompilerParams(collective_id=0, has_side_effects=True),
         name="richardson",
     )(source, coeffs, row_factor, col_factor, tile_mask, *constants)
-    return result, norms[:, 0]
+    return result, norms[0, 0:ITERS]
 
 
 def solution(mesh):

time: 76.2 us -> 74.7 us (0.980)
  Pallas kernels: 74.2 us -> 72.8 us
    pallas_call x1, Pallas kernels: 74.2 us -> 72.8 us  [local_step(): pl.pallas_call(functools.partial(kernel, sizes), out_shape=(pltpu.VMEM((R...]
where the time goes in v3:
time: 74.7 us; the launch traced here: 74.6 us
  Pallas kernels  72.8 us (97%)
  local copies, waits for them, and re-layouts  1.13 us (2%)
    pallas_call x1, Pallas kernels, local_step(): pl.pallas_call(functools.partial(kernel, sizes), out_shape=(pltpu.VMEM((R...  72.8 us

profile of v3, /device:TPU:1, one launch (start us, length us, event | category | flops | bytes accessed | tf_op | source)
XLA Modules:
  0.0 74.6 jit_solution(1957945102315470905)
XLA Ops:
  0.6 72.8 %richardson.1 = (f32[64,128]{1,0:T(8,128)S(1)}, f32[1,128]{1,0:T(1,128)S(1)}) custom-call(f32[64,128]{1,0:T(8,128)} %source_hbm.1, f32[65,65]{1,0:T(8,128)} %coeffs_hbm.1, f32[64,2048]{1,0:T(8,128)} %row_hbm.1, f32[2048,128]{1,0:T(8,128)} %col_hbm.1, s32[8,8]{1,0:T(8,128)} %mask_hbm.1, bf16[512,256]{1,0:T(8,128)(2,1)} %constant.10.clone.col_forward_hbm, ...), custom_call_target="tpu_custom_call" | custom-call | tf_op jit(solution)/shard_map/richardson/pallas_call | solution.py:505
  73.4 0.6 copy.13
  74.1 0.5 slice_bitcast_fusion

commit v4 on v3

--- a/solution.py
+++ b/solution.py
@@ -21,7 +21,6 @@
 NEAR = 1
 STEP = 0.25
 TINY = 1e-06
-Z_SIZE = 8
 MESH = pl.DeviceIdType.MESH
 F32 = jnp.float32
 BF16 = jnp.bfloat16
@@ -117,6 +116,10 @@
     return below(*parts_re), below(*parts_im)
 
 
+def around(index, size):
+    return jnp.where(index >= size, index - size, index)
+
+
 def parts(ref):
     half = ref.shape[0] // 2
     return ref[0:half, :], ref[half:, :]
@@ -135,14 +138,11 @@
     mixed_send_sem, mixed_recv_sem, sum_send, sum_y_recv, sum_x_recv,
 ):
     n_hx, n_hy = sizes
-    n_z = min(n_hx, Z_SIZE)
-    n_x = n_hx // n_z
     hx, hy = lax.axis_index("hx"), lax.axis_index("hy")
     place = lax.rem(hx, GROUP)
     first = hx - place
     tile_row, tile_col = hx // GROUP, hy // 2
     core = lax.rem(hy, 2)
-    x, z = hx // n_z, lax.rem(hx, n_z)
     up, down, left, right = hx > 0, hx < n_hx - 1, hy > 0, hy < n_hy - 1
     own_rows = pl.ds(pl.multiple_of(BAND + place * ROWS, BAND), ROWS)
     own_far = pl.ds(pl.multiple_of(lax.rem(place, 2) * ROWS, ROWS), ROWS)
@@ -181,25 +181,18 @@
         pl.semaphore_signal(barrier, inc=1, device_id=(to_hx, to_hy), device_id_type=MESH)
 
     def greet_y(i, carry):
-        greet(hx, lax.rem(hy + i, n_hy))
+        greet(hx, around(hy + i, n_hy))
         return carry
 
-    def greet_z(i, carry):
-        greet(x * n_z + lax.rem(z + i, n_z), hy)
+    def greet_x(i, carry):
+        greet(around(hx + i, n_hx), hy)
         return carry
 
-    def greet_x(i, carry):
-        greet(lax.rem(x + i, n_x) * n_z + z, hy)
-        return carry
-
-    lax.fori_loop(1, n_hy, greet_y, 0)
-    lax.fori_loop(1, n_z, greet_z, 0)
-    lax.fori_loop(1, n_x, greet_x, 0)
+    lax.fori_loop(1, n_hx, greet_x, 0, unroll=4)
+    lax.fori_loop(1, n_hy, greet_y, 0, unroll=4)
     for there, to_hx in ((up, hx - 1), (down, hx + 1)):
         @pl.when(there)
         def _():
-            greet(to_hx, hy)
-
             @pl.when(left)
             def _():
                 greet(to_hx, hy - 1)
@@ -249,8 +242,8 @@
         col_parts[which, COLS:, :] = beside(high, low)
 
     count = (up.astype(jnp.int32) + down.astype(jnp.int32)) * (
-        1 + left.astype(jnp.int32) + right.astype(jnp.int32)
-    ) + (n_hy - 1 + n_z - 1 + n_x - 1)
+        left.astype(jnp.int32) + right.astype(jnp.int32)
+    ) + (n_hy - 1 + n_hx - 1)
     pl.semaphore_wait(barrier, count)
 
     def prepare():
@@ -439,17 +432,17 @@
             )
 
         def start(i, carry):
-            copy(lax.rem(index + i, size), index).start()
+            copy(around(index + i, size), index).start()
             return carry
 
         def wait(i, carry):
-            other = lax.rem(index + i, size)
+            other = around(index + i, size)
             item = remote(held.at[other], held.at[other], sum_send.at[other], recv_sem.at[other], *device(other))
             item.wait_recv()
             copy(other, index).wait_send()
             return carry
 
-        lax.fori_loop(1, size, start, 0)
+        lax.fori_loop(1, size, start, 0, unroll=4)
         lax.fori_loop(1, size, wait, 0)
         return jnp.sum(held[...], axis=0)
 
@@ -457,9 +450,7 @@
     sums = jnp.sum(squares[ITERS:, :], axis=1, keepdims=True)
     total = jnp.sum(jnp.where(row == col, sums, 0.0), axis=0, keepdims=True)
     total = gather(total, sum_y, sum_y_recv, hy, n_hy, lambda to: (hx, to))
-    total = gather(total, sum_x.at[0:n_z], sum_x_recv.at[0], z, n_z, lambda to: (x * n_z + to, hy))
-    if n_x > 1:
-        total = gather(total, sum_x.at[n_z : n_z + n_x], sum_x_recv.at[1], x, n_x, lambda to: (to * n_z + z, hy))
+    total = gather(total, sum_x, sum_x_recv, hx, n_hx, lambda to: (to, hy))
     norm_ref[...] = jnp.sqrt(total / (ROWS * COLS * n_hx * n_hy) + TINY)
 
 
@@ -500,7 +491,7 @@
         dma((2, 2)), dma((2, 2)),
         dma((2, 2, 3)), dma((2, 2, 3)),
         dma((2,)), dma((2,)),
-        dma((max(n_hy, n_hx),)), dma((n_hy,)), dma((2, n_hx)),
+        dma((max(n_hy, n_hx),)), dma((n_hy,)), dma((n_hx,)),
     ]
     result, norms = pl.pallas_call(
         functools.partial(kernel, sizes),

time: 74.7 us -> 73.4 us (0.983)
  Pallas kernels: 72.8 us -> 71.5 us
    pallas_call x1, Pallas kernels: 72.8 us -> 71.5 us  [local_step(): pl.pallas_call(functools.partial(kernel, sizes), out_shape=(pltpu.VMEM((R...]
where the time goes in v4:
time: 73.4 us; the launch traced here: 73.2 us
  Pallas kernels  71.5 us (97%)
  local copies, waits for them, and re-layouts  1.13 us (2%)
    pallas_call x1, Pallas kernels, local_step(): pl.pallas_call(functools.partial(kernel, sizes), out_shape=(pltpu.VMEM((R...  71.5 us

profile of v4, /device:TPU:1, one launch (start us, length us, event | category | flops | bytes accessed | tf_op | source)
XLA Modules:
  0.0 73.2 jit_solution(7954581736039822363)
XLA Ops:
  0.6 71.5 %richardson.1 = (f32[64,128]{1,0:T(8,128)S(1)}, f32[1,128]{1,0:T(1,128)S(1)}) custom-call(f32[64,128]{1,0:T(8,128)} %source_hbm.1, f32[65,65]{1,0:T(8,128)} %coeffs_hbm.1, f32[64,2048]{1,0:T(8,128)} %row_hbm.1, f32[2048,128]{1,0:T(8,128)} %col_hbm.1, s32[8,8]{1,0:T(8,128)} %mask_hbm.1, bf16[512,256]{1,0:T(8,128)(2,1)} %constant.10.clone.col_forward_hbm, ...), custom_call_target="tpu_custom_call" | custom-call | tf_op jit(solution)/shard_map/richardson/pallas_call | solution.py:496
  72.1 0.6 copy.13
  72.7 0.5 slice_bitcast_fusion

commit v5 on v4

--- a/solution.py
+++ b/solution.py
@@ -379,7 +379,9 @@
         pl.when(k == 0)(prepare)
 
         tile_waits(slot, True)
-        mixed = dot_deep(row_near[...], beside(*split(field[slot, BAND : BAND + TILE, :])))
+        near_high, near_low = parts(row_near)
+        high, low = split(field[slot, BAND : BAND + TILE, :])
+        mixed = dot(near_high, high) + dot(near_high, low) + dot(near_low, high)
         mixed_send[slot] = mixed
         mixed_copy(slot).start()
         total = dot_small(beside(*split(mixed)), col_parts[0])

time: 73.4 us -> 73.4 us (level)
  no operation moved by 1% of the time
where the time goes in v5:
time: 73.4 us; the launch traced here: 73.2 us
  Pallas kernels  71.5 us (97%)
  local copies, waits for them, and re-layouts  1.13 us (2%)
    pallas_call x1, Pallas kernels, local_step(): pl.pallas_call(functools.partial(kernel, sizes), out_shape=(pltpu.VMEM((R...  71.5 us

profile of v5, /device:TPU:1, one launch (start us, length us, event | category | flops | bytes accessed | tf_op | source)
XLA Modules:
  0.0 73.2 jit_solution(1996673729328181290)
XLA Ops:
  0.6 71.5 %richardson.1 = (f32[64,128]{1,0:T(8,128)S(1)}, f32[1,128]{1,0:T(1,128)S(1)}) custom-call(f32[64,128]{1,0:T(8,128)} %source_hbm.1, f32[65,65]{1,0:T(8,128)} %coeffs_hbm.1, f32[64,2048]{1,0:T(8,128)} %row_hbm.1, f32[2048,128]{1,0:T(8,128)} %col_hbm.1, s32[8,8]{1,0:T(8,128)} %mask_hbm.1, bf16[512,256]{1,0:T(8,128)(2,1)} %constant.10.clone.col_forward_hbm, ...), custom_call_target="tpu_custom_call" | custom-call | tf_op jit(solution)/shard_map/richardson/pallas_call | solution.py:498
  72.1 0.6 copy.13
  72.7 0.5 slice_bitcast_fusion
